TPU v7x, 32 devices: a whole 2x2x4 slice. The times are simulated.
32 devices in a mesh: tm: 4 (over y, x), region: 8 (over z, core).
Axes of the slice: x: 2, y: 2, z: 4, core: 2. Of those that a mesh axis runs over, the one named last changes fastest.
Arguments:
- gen: float32 [8, 128, 4, 128], P('region', None, 'tm'), may hold values from 0 to 1
- flow: float32 [32, 128, 4, 128], P('region', None, 'tm'), may hold values from -4 to 4
- price: float32 [32, 128, 4, 128], P('region', None, 'tm'), may hold values from -6 to 6
- ramp_dual: float32 [8, 128, 4, 128], P('region', None, 'tm'), may hold values from -3 to 3
- demand: float32 [32, 128, 4, 128], P('region', None, 'tm'), may hold values from -6 to 6
- incid_tiles: bfloat16 [256, 128, 128], P('region'), may hold values from -0.1875 to 0.1875
- tile_bus: int32 [256], P('region'), may hold values from 0 to 3
- tile_line: int32 [256], P('region'), may hold values from 0 to 31, as said below
- gen_tiles: bfloat16 [8, 128, 128], P('region'), may hold values from -0.5 to 0.5
- gen_bus: int32 [8], P('region'), may hold values from 0 to 3
- gen_cost: float32 [8, 128], P('region'), may hold values from 0.1 to 1
- gen_cap: float32 [8, 128], P('region'), may hold values from 0.5 to 2
- ramp_cap: float32 [8, 128], P('region'), may hold values from 0.05 to 0.5
- flow_cap: float32 [32, 128], P('region'), may hold values from 0.3 to 1.5
- weight: float32 [], replicated, may hold values from 0.5 to 2
Outputs:
- gen_next: float32 [8, 128, 4, 128], P('region', None, 'tm')
- flow_next: float32 [32, 128, 4, 128], P('region', None, 'tm')
- price_next: float32 [32, 128, 4, 128], P('region', None, 'tm')
- ramp_next: float32 [8, 128, 4, 128], P('region', None, 'tm')
Inputs may be any that keep to these rules, and one draw needn't show every extreme that they name: Tile t belongs to region r = t // 32; its line block lies in region r - 1, r or r + 1 (those that exist), where region q holds line blocks q * 4 to (q + 1) * 4 - 1. No two tiles have the same pair (tile_bus, tile_line) within a region.
All inputs are finite; a program needn't handle non-finite values.
Results may differ from a plain program's by a relative error of at most 0.0006.
The roundings to bfloat16 on the way count: a program that leaves them out, or rounds other values in their place, can miss the bound.
Values may be sent and summed in bfloat16 or wider, within the bound.
A program may use at most 64 MiB of HBM per device.

v0:
```python
import jax
import jax.numpy as jnp
from jax import lax
from jax.sharding import PartitionSpec as P

step_scale = 0.4
tiny = 1e-06


def shifted(value, axis, steps):
    count = lax.axis_size(axis)
    initial, last = (max(0, -steps), min(count, count - steps))
    return lax.ppermute(value, axis, [(source, source + steps) for source in range(initial, last)])


def with_halo(cells, sides, width):
    for axis, dim in sides:
        count = lax.axis_size(axis)
        ends = count - 1
        head = lax.slice_in_dim(cells, 0, width, axis=dim)
        tail = lax.slice_in_dim(cells, cells.shape[dim] - width, cells.shape[dim], axis=dim)
        cells = jnp.concatenate(
            [
                lax.ppermute(tail, axis, [(i, (i + 1) % count) for i in range(ends)]),
                cells,
                lax.ppermute(head, axis, [((i + 1) % count, i) for i in range(ends)]),
            ],
            axis=dim,
        )
    return cells


def from_behind(value, axis, steps):
    count = lax.axis_size(axis)
    pairs = [(source, (source + steps) % count) for source in range(count)]
    return lax.ppermute(value, axis, pairs)


def shards(
    gen,
    flow,
    price,
    ramp_dual,
    demand,
    incid_tiles,
    tile_bus,
    tile_line,
    gen_tiles,
    gen_bus,
    gen_cost,
    gen_cap,
    ramp_cap,
    flow_cap,
    weight,
):
    gen_blocks, block, hours, scenarios = gen.shape
    line_blocks = flow.shape[0]
    bus_blocks = price.shape[0]
    columns = hours * scenarios
    region = lax.axis_index("region")
    rel_block = tile_line - (region - 1) * line_blocks

    def pull_lines(price_now):
        price_low = price_now.astype(jnp.bfloat16).reshape(bus_blocks, block, columns)
        picked = price_low[tile_bus]
        contrib = jnp.einsum(
            "tji,tjc->tic", incid_tiles, picked, preferred_element_type=jnp.float32
        )
        window_sum = jax.ops.segment_sum(contrib, rel_block, num_segments=3 * line_blocks)
        own_part = window_sum[line_blocks : 2 * line_blocks]
        lower_part = window_sum[:line_blocks]
        upper_part = window_sum[2 * line_blocks :]
        from_above = shifted(lower_part, "region", -1)
        from_below = shifted(upper_part, "region", 1)
        line_pull = own_part + from_above + from_below
        gen_picked = price_low[gen_bus]
        gen_pull = jnp.einsum(
            "gji,gjc->gic", gen_tiles, gen_picked, preferred_element_type=jnp.float32
        )
        return (
            line_pull.reshape(line_blocks, block, hours, scenarios),
            gen_pull.reshape(gen_blocks, block, hours, scenarios),
        )

    def push_buses(flow_bar, gen_bar):
        flow_low = flow_bar.astype(jnp.bfloat16).reshape(line_blocks, block, columns)
        window = with_halo(flow_low, (("region", 0),), line_blocks)
        picked = window[rel_block]
        contrib = jnp.einsum(
            "tij,tjc->tic", incid_tiles, picked, preferred_element_type=jnp.float32
        )
        bus_sum = jax.ops.segment_sum(contrib, tile_bus, num_segments=bus_blocks)
        gen_low = gen_bar.astype(jnp.bfloat16).reshape(gen_blocks, block, columns)
        gen_contrib = jnp.einsum(
            "gij,gjc->gic", gen_tiles, gen_low, preferred_element_type=jnp.float32
        )
        bus_sum = bus_sum + jax.ops.segment_sum(gen_contrib, gen_bus, num_segments=bus_blocks)
        return bus_sum.reshape(bus_blocks, block, hours, scenarios)

    def back_term(dual_now):
        next_first = from_behind(dual_now[:, :, 0, :], "tm", -1)
        later = jnp.concatenate([dual_now[:, :, 1:, :], next_first[:, :, None, :]], axis=2)
        return dual_now - later

    def ramp_term(gen_bar):
        prev_last = from_behind(gen_bar[:, :, hours - 1, :], "tm", 1)
        earlier = jnp.concatenate([prev_last[:, :, None, :], gen_bar[:, :, : hours - 1, :]], axis=2)
        return gen_bar - earlier

    def primal_step(state, step_primal):
        gen_now, flow_now, price_now, dual_now = state
        line_pull, gen_pull = pull_lines(price_now)
        grad_gen = gen_cost[:, :, None, None] - gen_pull + back_term(dual_now)
        gen_new = jnp.clip(gen_now - step_primal * grad_gen, 0.0, gen_cap[:, :, None, None])
        limit = flow_cap[:, :, None, None]
        flow_new = jnp.clip(flow_now + step_primal * line_pull, -limit, limit)
        return (gen_new, flow_new)

    def dual_step(state, gen_new, flow_new, step_dual):
        gen_now, flow_now, price_now, dual_now = state
        gen_bar = 2.0 * gen_new - gen_now
        flow_bar = 2.0 * flow_new - flow_now
        pushed = push_buses(flow_bar, gen_bar)
        ramping = ramp_term(gen_bar)
        price_new = price_now + step_dual * (demand - pushed)
        lifted = dual_now + step_dual * ramping
        bound = ramp_cap[:, :, None, None]
        dual_new = lifted - step_dual * jnp.clip(lifted / step_dual, -bound, bound)
        return (price_new, dual_new)

    state = (gen, flow, price, ramp_dual)
    gen_one, flow_one = primal_step(state, step_scale / weight)
    primal_sq = jnp.sum((gen_one - gen) ** 2) + jnp.sum((flow_one - flow) ** 2)
    primal_total = lax.psum(primal_sq, ("tm", "region"))
    price_one, dual_one = dual_step(state, gen_one, flow_one, step_scale * weight)
    dual_sq = jnp.sum((price_one - price) ** 2) + jnp.sum((dual_one - ramp_dual) ** 2)
    dual_total = lax.psum(dual_sq, ("tm", "region"))
    devices_all = lax.axis_size("tm") * lax.axis_size("region")
    primal_mean = primal_total / ((gen.size + flow.size) * devices_all)
    dual_mean = dual_total / ((price.size + ramp_dual.size) * devices_all)
    weight_two = jnp.sqrt(weight * jnp.sqrt((dual_mean + tiny) / (primal_mean + tiny)))
    state_one = (gen_one, flow_one, price_one, dual_one)
    gen_two, flow_two = primal_step(state_one, step_scale / weight_two)
    price_two, dual_two = dual_step(state_one, gen_two, flow_two, step_scale * weight_two)
    return (gen_two, flow_two, price_two, dual_two)


def solution(mesh):
    placed = (
        P("region", None, "tm", None),
        P("region", None, "tm", None),
        P("region", None, "tm", None),
        P("region", None, "tm", None),
        P("region", None, "tm", None),
        P("region", None, None),
        P("region"),
        P("region"),
        P("region", None, None),
        P("region"),
        P("region", None),
        P("region", None),
        P("region", None),
        P("region", None),
        P(),
    )
    return jax.shard_map(
        shards,
        mesh=mesh,
        in_specs=placed,
        out_specs=(
            P("region", None, "tm", None),
            P("region", None, "tm", None),
            P("region", None, "tm", None),
            P("region", None, "tm", None),
        ),
        check_vma=False,
    )
```

profile of v0, /device:TPU:0, one launch (start us, length us, event | category | flops | bytes accessed | tf_op | source)
XLA Modules:
  0.0 130.7 jit_solution(5818173558093201576)
XLA Ops:
  0.6 0.0 copy-start
  0.7 0.8 compare_select_fusion
  1.4 1.1 convert_element_type.18
  2.6 1.7 %gather_fusion = bf16[32,128,128]{2,1,0:T(8,128)(2,1)} fusion(bf16[4,128,128]{2,1,0:T(8,128)(2,1)S(1)} %bitcast.167, s32[1024]{0:T(1024)S(1)} %pad_clamp_fusion.1), kind=kCustom, calls=%fused_computation | custom fusion | bytes 2097280 | tf_op jit(solution)/shard_map/gather | solution.py:65
  4.2 1.7 %convolution_bitcast_fusion.3 = f32[32,128,128]{1,2,0:T(8,128)S(1)} fusion(bf16[32,128,128]{2,1,0:T(8,128)(2,1)} %gather_fusion, bf16[32,128,128]{2,1,0:T(8,128)(2,1)S(1)} %copy-done), kind=kOutput, calls=%fused_computation.11 | convolution fusion | flops 134217728 | bytes 4194304 | tf_op jit(solution)/shard_map/tji,tjc->tic/dot_general | solution.py:66
  6.0 1.8 %copy.23 = f32[32,128,128]{2,1,0:T(8,128)} copy(f32[32,128,128]{1,2,0:T(8,128)S(1)} %convolution_bitcast_fusion.3) | data formatting | bytes 4194304 | tf_op jit(solution)/shard_map/tji,tjc->tic/dot_general | solution.py:66
  7.8 0.1 broadcast.79.clone
  7.9 0.0 copy-start.7
  8.0 0.0 copy-start.20
  8.0 0.0 copy-start.13
  8.0 0.0 copy-start.15
  8.0 4.7 %scatter_fusion = f32[12,128,128]{2,1,0:T(8,128)S(1)} fusion(f32[12,128,128]{2,1,0:T(8,128)S(1)} %broadcast.79.clone, s32[32]{0:T(128)S(1)} %get-tuple-element.67, f32[32,128,128]{2,1,0:T(8,128)} %copy.23), kind=kCustom, calls=%fused_computation.4 | custom fusion | flops 524288 | bytes 6291584 | tf_op jit(solution)/shard_map/scatter-add | solution.py:69
  12.7 0.0 copy-start.4
  12.7 0.7 fusion.57
  13.4 1.3 collective-permute-start.1
  14.7 3.7 %collective-permute-start.2 = (f32[4,128,128]{2,1,0:T(8,128)S(1)}, f32[4,128,128]{2,1,0:T(8,128)}, u32[]{:S(2)}, u32[]{:S(2)}) collective-permute-start(f32[4,128,128]{2,1,0:T(8,128)S(1)} %get-tuple-element.71), channel_id=1, source_target_pairs={{0,1},{1,2},{2,3},{3,4},{4,5},{5,6},{6,7},{8,9},{9,10},{10,11},{11... | collective-permute-start | bytes 786440 | tf_op jit(solution)/shard_map/ppermute | solution.py:13
  18.5 0.1 copy.20
  18.6 4.0 %collective-permute-start = (f32[1,128,128]{1,2,0:T(8,128)S(1)}, f32[1,128,128]{1,2,0:T(8,128)S(1)}, u32[]{:S(2)}, u32[]{:S(2)}) collective-permute-start(f32[1,128,128]{1,2,0:T(8,128)S(1)} %bitcast.173), channel_id=1, source_target_pairs={{0,24},{8,0},{16,8},{24,16},{1,25},{9,1},{17,9},{25,17},{2,26},{10... | collective-permute-start | bytes 196616 | tf_op jit(solution)/shard_map/ppermute | solution.py:36
  23.9 0.1 constant_dynamic-slice_fusion
  24.0 0.1 copy.21
  24.1 0.8 and_reduce_fusion
  24.9 0.2 fusion.35
  25.1 0.6 multiply_reduce_fusion.2
  25.8 2.1 %collective-permute-start.5 = (f32[1,128,128]{1,2,0:T(8,128)S(1)}, f32[1,128,128]{1,2,0:T(8,128)S(1)}, u32[]{:S(2)}, u32[]{:S(2)}) collective-permute-start(f32[1,128,128]{1,2,0:T(8,128)S(1)} %get-tuple-element.73), channel_id=1, source_target_pairs={{0,8},{8,16},{16,24},{24,0},{1,9},{9,17},{17,25},{25,1},{2,10},{10... | collective-permute-start | bytes 196616 | tf_op jit(solution)/shard_map/ppermute | solution.py:36
  27.9 1.8 %multiply_reduce_fusion = (f32[]{:T(128)}, f32[4,128,1,128]{3,1,0,2:T(8,128)S(1)}) fusion(f32[4,128,1,128]{3,1,0,2:T(8,128)S(1)} %bitcast.171, f32[4,128,128]{2,1,0:T(8,128)} %collective-permute-done.2, f32[4,128,128]{2,1,0:T(8,128)S(1)} %collective-permute-done.1, f32[12,128,128]{2,1,0:T(8,128)S(1)} %scatter_fusion, f32[]{:T(128)S(6)} %div.23, ...), kind=kLoop, calls=%fused_computation.42 | loop fusion | flops 589823 | bytes 1314824 | tf_op jit(solution)/shard_map/reduce_sum | solution.py:133
  29.7 1.3 collective-permute-start.3
  31.0 1.3 collective-permute-start.4
  32.3 2.0 %multiply_reduce_fusion.3 = (f32[]{:T(128)}, f32[1,128,1,128]{1,3,2,0:T(8,128)}) fusion(f32[1,128,1,128]{1,3,2,0:T(8,128)S(1)} %copy.20, f32[128]{0:T(128)S(1)} %bitcast_negate_fusion, f32[128]{0:T(128)} %bitcast.180, f32[1,128,128]{1,2,0:T(8,128)S(1)} %collective-permute-done.5, f32[1,128,1,128]{1,3,2,0:T(8,128)S(1)} %copy.21, ...), kind=kLoop, calls=%fused_computation.70 | loop fusion | flops 212991 | bytes 328712 | tf_op jit(solution)/shard_map/reduce_sum | solution.py:136
  34.3 1.4 %collective-permute-start.6 = (f32[1,128,128]{1,2,0:T(8,128)}, f32[1,128,128]{1,2,0:T(8,128)}, u32[]{:S(2)}, u32[]{:S(2)}) collective-permute-start(f32[1,128,128]{1,2,0:T(8,128)} %bitcast.30), channel_id=1, source_target_pairs={{0,24},{8,0},{16,8},{24,16},{1,25},{9,1},{17,9},{25,17},{2,26},{10... | collective-permute-start | bytes 196616 | tf_op jit(solution)/shard_map/ppermute | solution.py:36
  37.0 0.7 gather_fusion.1
  37.8 2.2 %convolution_bitcast_fusion.2 = f32[32,128,128]{1,2,0:T(8,128)} fusion(bf16[32,128,128]{2,1,0:T(8,128)(2,1)S(1)} %gather_fusion.1, bf16[32,128,128]{2,1,0:T(8,128)(2,1)S(1)} %copy-done), kind=kOutput, calls=%fused_computation.10 | convolution fusion | flops 134217728 | bytes 4194304 | tf_op jit(solution)/shard_map/tij,tjc->tic/dot_general | solution.py:89
  40.0 1.9 %copy.27 = f32[32,128,128]{2,1,0:T(8,128)S(1)} copy(f32[32,128,128]{1,2,0:T(8,128)} %convolution_bitcast_fusion.2) | data formatting | bytes 4194304 | tf_op jit(solution)/shard_map/tij,tjc->tic/dot_general | solution.py:89
  42.0 2.8 %scatter_fusion.1 = f32[4,128,128]{2,1,0:T(8,128)S(1)} fusion(f32[4,128,128]{2,1,0:T(8,128)S(1)} %broadcast.78.clone, s32[32]{0:T(128)} %param.25, f32[32,128,128]{2,1,0:T(8,128)S(1)} %copy.27), kind=kCustom, calls=%fused_computation.5 | custom fusion | flops 524288 | bytes 6291584 | tf_op jit(solution)/shard_map/scatter-add | solution.py:92
  44.8 0.1 copy.55
  44.9 1.6 %fusion.5 = f32[1,128,1,128]{1,3,2,0:T(8,128)S(1)} fusion(f32[1,128,128]{1,2,0:T(8,128)S(1)} %copy.55, bf16[1,128,128]{2,1,0:T(8,128)(2,1)} %param.27, pred[]{:T(512)} %and_reduce_fusion, f32[1,128,1,128]{1,3,2,0:T(8,128)S(1)} %copy.21, f32[1,128,1,128]{1,3,2,0:T(8,128)S(1)} %fusion.35), kind=kOutput, calls=%fused_computation.21 | convolution fusion | flops 4276224 | bytes 294913 | tf_op jit(solution)/shard_map/gij,gjc->gic/dot_general | solution.py:94
  46.5 0.1 copy.30
  46.6 1.7 %multiply_reduce_fusion.1 = (f32[]{:T(128)}, f32[4,128,1,128]{3,1,0,2:T(8,128)S(1)}) fusion(f32[4,128,1,128]{3,1,0,2:T(8,128)} %bitcast.168, f32[4,128,1,128]{3,1,0,2:T(8,128)} %bitcast.169, f32[4,128,1,128]{3,1,0,2:T(8,128)S(1)} %constant_dynamic-update-slice_fusion.1, f32[]{:T(128)S(6)} %mul.88), kind=kLoop, calls=%fused_computation.43 | loop fusion | flops 393215 | bytes 1048584 | tf_op jit(solution)/shard_map/reduce_sum | solution.py:136
  48.3 0.7 copy-done.1
  49.0 1.7 %gather_fusion.2 = bf16[32,128,128]{2,1,0:T(8,128)(2,1)} fusion(bf16[4,128,128]{2,1,0:T(8,128)(2,1)S(1)} %convert_bitcast_fusion, s32[1024]{0:T(1024)S(1)} %pad_clamp_fusion.1), kind=kCustom, calls=%fused_computation.2 | custom fusion | bytes 2097280 | tf_op jit(solution)/shard_map/gather | solution.py:65
  50.7 1.7 %convolution_bitcast_fusion.1 = f32[32,128,128]{1,2,0:T(8,128)S(1)} fusion(bf16[32,128,128]{2,1,0:T(8,128)(2,1)} %gather_fusion.2, bf16[32,128,128]{2,1,0:T(8,128)(2,1)S(1)} %copy-done), kind=kOutput, calls=%fused_computation.9 | convolution fusion | flops 134217728 | bytes 4194304 | tf_op jit(solution)/shard_map/tji,tjc->tic/dot_general | solution.py:66
  52.4 1.8 %copy.39 = f32[32,128,128]{2,1,0:T(8,128)} copy(f32[32,128,128]{1,2,0:T(8,128)S(1)} %convolution_bitcast_fusion.1) | data formatting | bytes 4194304 | tf_op jit(solution)/shard_map/tji,tjc->tic/dot_general | solution.py:66
  54.3 0.1 broadcast.79
  54.4 0.0 copy-start.6
  54.4 4.7 %scatter_fusion.2 = f32[12,128,128]{2,1,0:T(8,128)S(1)} fusion(f32[12,128,128]{2,1,0:T(8,128)S(1)} %broadcast.79, s32[32]{0:T(128)S(1)} %copy-done.12, f32[32,128,128]{2,1,0:T(8,128)} %copy.39), kind=kCustom, calls=%fused_computation.6 | custom fusion | flops 524288 | bytes 6291584 | tf_op jit(solution)/shard_map/scatter-add | solution.py:69
  59.1 1.3 collective-permute-start.7
  60.4 4.7 %collective-permute-start.8 = (f32[4,128,128]{2,1,0:T(8,128)S(1)}, f32[4,128,128]{2,1,0:T(8,128)S(1)}, u32[]{:S(2)}, u32[]{:S(2)}) collective-permute-start(f32[4,128,128]{2,1,0:T(8,128)S(1)} %get-tuple-element.69), channel_id=1, source_target_pairs={{0,1},{1,2},{2,3},{3,4},{4,5},{5,6},{6,7},{8,9},{9,10},{10,11},{11... | collective-permute-start | bytes 786440 | tf_op jit(solution)/shard_map/ppermute | solution.py:13
  66.4 0.2 fusion.1
  66.6 40.5 %all-reduce = (f32[]{:T(128)}, f32[]{:T(128)}) all-reduce(f32[]{:T(128)S(6)} %add.101, f32[]{:T(128)S(6)} %add.103), channel_id=1, replica_groups=mesh['tm'=4,'region'=8] {'tm','region'}, use_global_device_ids=true, to_apply=%region_5.6 | all-reduce | flops 2 | bytes 16 | tf_op jit(solution)/shard_map/psum | solution.py:137
  108.6 0.9 fusion.52
  109.5 2.3 %collective-permute-start.11 = (f32[1,128,128]{1,2,0:T(8,128)S(1)}, f32[1,128,128]{1,2,0:T(8,128)S(1)}, u32[]{:S(2)}, u32[]{:S(2)}) collective-permute-start(f32[1,128,128]{1,2,0:T(8,128)S(1)} %get-tuple-element.56), channel_id=1, source_target_pairs={{0,8},{8,16},{16,24},{24,0},{1,9},{9,17},{17,25},{25,1},{2,10},{10... | collective-permute-start | bytes 196616 | tf_op jit(solution)/shard_map/ppermute | solution.py:36
  111.8 0.7 copy.45
  112.5 0.9 fusion.21
  113.4 1.3 collective-permute-start.10
  114.7 3.0 %collective-permute-start.9 = (bf16[4,128,128]{2,1,0:T(8,128)(2,1)S(1)}, bf16[4,128,128]{2,1,0:T(8,128)(2,1)S(1)}, u32[]{:S(2)}, u32[]{:S(2)}) collective-permute-start(bf16[4,128,128]{2,1,0:T(8,128)(2,1)S(1)} %get-tuple-element.58), channel_id=1, source_target_pairs={{0,1},{1,2},{2,3},{3,4},{4,5},{5,6},{6,7},{8,9},{9,10},{10,11},{11... | collective-permute-start | bytes 393224 | tf_op jit(solution)/shard_map/ppermute | solution.py:24
  117.8 0.9 multiply_subtract_fusion
  118.7 0.7 copy.48
  119.5 0.7 gather_fusion.3
  120.2 2.2 %convolution_bitcast_fusion = f32[32,128,128]{1,2,0:T(8,128)} fusion(bf16[32,128,128]{2,1,0:T(8,128)(2,1)S(1)} %gather_fusion.3, bf16[32,128,128]{2,1,0:T(8,128)(2,1)S(1)} %copy-done), kind=kOutput, calls=%fused_computation.8 | convolution fusion | flops 134217728 | bytes 4194304 | tf_op jit(solution)/shard_map/tij,tjc->tic/dot_general | solution.py:89
  122.4 1.9 %copy.41 = f32[32,128,128]{2,1,0:T(8,128)S(1)} copy(f32[32,128,128]{1,2,0:T(8,128)} %convolution_bitcast_fusion) | data formatting | bytes 4194304 | tf_op jit(solution)/shard_map/tij,tjc->tic/dot_general | solution.py:89
  124.4 2.7 %scatter_fusion.3 = f32[4,128,128]{2,1,0:T(8,128)S(1)} fusion(f32[4,128,128]{2,1,0:T(8,128)S(1)} %broadcast.78, s32[32]{0:T(128)S(1)} %copy-done.10, f32[32,128,128]{2,1,0:T(8,128)S(1)} %copy.41), kind=kCustom, calls=%fused_computation.7 | custom fusion | flops 524288 | bytes 6291584 | tf_op jit(solution)/shard_map/scatter-add | solution.py:92
  127.1 0.1 copy.56
  127.2 1.6 %fusion.7 = f32[1,128,1,128]{1,3,2,0:T(8,128)S(1)} fusion(f32[1,128,128]{1,2,0:T(8,128)S(1)} %copy.56, bf16[1,128,128]{2,1,0:T(8,128)(2,1)} %param.27, pred[]{:T(512)} %and_reduce_fusion, f32[1,128,1,128]{1,3,2,0:T(8,128)S(1)} %fusion.35, f32[1,128,1,128]{1,3,2,0:T(8,128)S(1)} %get-tuple-element.57), kind=kOutput, calls=%fused_computation.23 | convolution fusion | flops 4276224 | bytes 294913 | tf_op jit(solution)/shard_map/gij,gjc->gic/dot_general | solution.py:94
  128.8 0.1 copy.43
  128.9 1.8 %multiply_add_fusion = f32[4,128,1,128]{3,1,0,2:T(8,128)} fusion(f32[4,128,1,128]{3,1,0,2:T(8,128)} %copy-done.1, f32[4,128,1,128]{3,1,0,2:T(8,128)} %bitcast.170, f32[4,128,1,128]{3,1,0,2:T(8,128)S(1)} %constant_dynamic-update-slice_fusion, f32[]{:T(128)S(6)} %mul.106), kind=kLoop, calls=%fused_computation.40 | loop fusion | flops 196608 | bytes 1048580 | tf_op jit(solution)/shard_map/add | solution.py:125
  (63 shorter events, 0.4 us)
Async XLA Ops:
  0.6 3.6 %copy-start = (bf16[32,128,128]{2,1,0:T(8,128)(2,1)S(1)}, bf16[32,128,128]{2,1,0:T(8,128)(2,1)}, u32[]{:S(2)}) copy-start(bf16[32,128,128]{2,1,0:T(8,128)(2,1)} %param.24) | copy-start | bytes 3145732
  1.4 6.5 %copy-start.11 = (s32[32]{0:T(128)}, s32[32]{0:T(128)S(1)}, u32[]{:S(2)}) copy-start(s32[32]{0:T(128)S(1)} %get-tuple-element.67) | copy-start | bytes 388
  7.9 10.5 %copy-start.7 = (f32[1,128,1,128]{3,2,1,0:T(1,128)S(1)}, f32[1,128,1,128]{3,2,1,0:T(1,128)}, u32[]{:S(2)}) copy-start(f32[1,128,1,128]{3,2,1,0:T(1,128)} %param.22) | copy-start | bytes 196612
  7.9 15.3 %copy-start.9 = (f32[4,128]{1,0:T(4,128)S(1)}, f32[4,128]{1,0:T(4,128)}, u32[]{:S(2)}) copy-start(f32[4,128]{1,0:T(4,128)} %param.32) | copy-start | bytes 6148
  7.9 16.0 %copy-start.8 = (f32[1,128,1,128]{3,2,1,0:T(1,128)S(1)}, f32[1,128,1,128]{3,2,1,0:T(1,128)}, u32[]{:S(2)}) copy-start(f32[1,128,1,128]{3,2,1,0:T(1,128)} %param.19) | copy-start | bytes 196612
  8.0 16.1 %copy-start.20 = (s32[3]{0:T(128)S(1)}, s32[3]{0:T(128)}, u32[]{:S(2)}) copy-start(s32[3]{0:T(128)} %constant.71.clone.1) | copy-start | bytes 40
  8.0 16.9 %copy-start.17 = (f32[1,128]{1,0:T(1,128)S(1)}, f32[1,128]{1,0:T(1,128)}, u32[]{:S(2)}) copy-start(f32[1,128]{1,0:T(1,128)} %param.31) | copy-start | bytes 1540
  8.0 16.9 %copy-start.5 = (bf16[1,128,128]{2,1,0:T(8,128)(2,1)S(1)}, bf16[1,128,128]{2,1,0:T(8,128)(2,1)}, u32[]{:S(2)}) copy-start(bf16[1,128,128]{2,1,0:T(8,128)(2,1)} %param.27) | copy-start | bytes 98308
  8.0 16.9 %copy-start.13 = (f32[1,128]{1,0:T(1,128)S(1)}, f32[1,128]{1,0:T(1,128)}, u32[]{:S(2)}) copy-start(f32[1,128]{1,0:T(1,128)} %param.29) | copy-start | bytes 1540
  8.0 16.9 %copy-start.15 = (f32[1,128]{1,0:T(1,128)S(1)}, f32[1,128]{1,0:T(1,128)}, u32[]{:S(2)}) copy-start(f32[1,128]{1,0:T(1,128)} %param.30) | copy-start | bytes 1540
  12.7 15.2 %copy-start.4 = (f32[4,128,1,128]{3,2,1,0:T(1,128)S(1)}, f32[4,128,1,128]{3,2,1,0:T(1,128)}, u32[]{:S(2)}) copy-start(f32[4,128,1,128]{3,2,1,0:T(1,128)} %param.20) | copy-start | bytes 786436
  13.4 14.4 %collective-permute-start.1 = (f32[4,128,128]{2,1,0:T(8,128)}, f32[4,128,128]{2,1,0:T(8,128)S(1)}, u32[]{:S(2)}, u32[]{:S(2)}) collective-permute-start(f32[4,128,128]{2,1,0:T(8,128)} %get-tuple-element.70), channel_id=1, source_target_pairs={{1,0},{2,1},{3,2},{4,3},{5,4},{6,5},{7,6},{9,8},{10,9},{11,10},{12... | collective-permute-start | bytes 786440 | tf_op jit(solution)/shard_map/ppermute | solution.py:13
  14.7 13.1 %collective-permute-start.2 = (f32[4,128,128]{2,1,0:T(8,128)S(1)}, f32[4,128,128]{2,1,0:T(8,128)}, u32[]{:S(2)}, u32[]{:S(2)}) collective-permute-start(f32[4,128,128]{2,1,0:T(8,128)S(1)} %get-tuple-element.71), channel_id=1, source_target_pairs={{0,1},{1,2},{2,3},{3,4},{4,5},{5,6},{6,7},{8,9},{9,10},{10,11},{11... | collective-permute-start | bytes 786440 | tf_op jit(solution)/shard_map/ppermute | solution.py:13
  18.6 6.3 %collective-permute-start = (f32[1,128,128]{1,2,0:T(8,128)S(1)}, f32[1,128,128]{1,2,0:T(8,128)S(1)}, u32[]{:S(2)}, u32[]{:S(2)}) collective-permute-start(f32[1,128,128]{1,2,0:T(8,128)S(1)} %bitcast.173), channel_id=1, source_target_pairs={{0,24},{8,0},{16,8},{24,16},{1,25},{9,1},{17,9},{25,17},{2,26},{10... | collective-permute-start | bytes 196616 | tf_op jit(solution)/shard_map/ppermute | solution.py:36
  24.9 12.9 %copy-start.19 = (f32[128]{0:T(128)}, f32[128]{0:T(128)S(1)}, u32[]{:S(2)}) copy-start(f32[128]{0:T(128)S(1)} %bitcast_negate_fusion) | copy-start | bytes 1540
  25.8 6.5 %collective-permute-start.5 = (f32[1,128,128]{1,2,0:T(8,128)S(1)}, f32[1,128,128]{1,2,0:T(8,128)S(1)}, u32[]{:S(2)}, u32[]{:S(2)}) collective-permute-start(f32[1,128,128]{1,2,0:T(8,128)S(1)} %get-tuple-element.73), channel_id=1, source_target_pairs={{0,8},{8,16},{16,24},{24,0},{1,9},{9,17},{17,25},{25,1},{2,10},{10... | collective-permute-start | bytes 196616 | tf_op jit(solution)/shard_map/ppermute | solution.py:36
  29.6 7.4 %copy-start.2 = (f32[4,128,1,128]{3,1,0,2:T(8,128)}, f32[4,128,1,128]{3,1,0,2:T(8,128)S(1)}, u32[]{:S(2)}) copy-start(f32[4,128,1,128]{3,1,0,2:T(8,128)S(1)} %get-tuple-element.61) | copy-start | bytes 786436
  29.7 7.3 %collective-permute-start.3 = (bf16[4,128,128]{2,1,0:T(8,128)(2,1)S(1)}, bf16[4,128,128]{2,1,0:T(8,128)(2,1)S(1)}, u32[]{:S(2)}, u32[]{:S(2)}) collective-permute-start(bf16[4,128,128]{2,1,0:T(8,128)(2,1)S(1)} %fusion.20), channel_id=1, source_target_pairs={{0,1},{1,2},{2,3},{3,4},{4,5},{5,6},{6,7},{8,9},{9,10},{10,11},{11... | collective-permute-start | bytes 393224 | tf_op jit(solution)/shard_map/ppermute | solution.py:24
  31.0 6.0 %collective-permute-start.4 = (bf16[4,128,128]{2,1,0:T(8,128)(2,1)S(1)}, bf16[4,128,128]{2,1,0:T(8,128)(2,1)S(1)}, u32[]{:S(2)}, u32[]{:S(2)}) collective-permute-start(bf16[4,128,128]{2,1,0:T(8,128)(2,1)S(1)} %fusion.20), channel_id=1, source_target_pairs={{1,0},{2,1},{3,2},{4,3},{5,4},{6,5},{7,6},{9,8},{10,9},{11,10},{12... | collective-permute-start | bytes 393224 | tf_op jit(solution)/shard_map/ppermute | solution.py:26
  34.3 74.3 %collective-permute-start.6 = (f32[1,128,128]{1,2,0:T(8,128)}, f32[1,128,128]{1,2,0:T(8,128)}, u32[]{:S(2)}, u32[]{:S(2)}) collective-permute-start(f32[1,128,128]{1,2,0:T(8,128)} %bitcast.30), channel_id=1, source_target_pairs={{0,24},{8,0},{16,8},{24,16},{1,25},{9,1},{17,9},{25,17},{2,26},{10... | collective-permute-start | bytes 196616 | tf_op jit(solution)/shard_map/ppermute | solution.py:36
  48.3 0.7 copy-start.1
  52.4 1.9 %copy-start.12 = (s32[32]{0:T(128)S(1)}, s32[32]{0:T(128)}, u32[]{:S(2)}) copy-start(s32[32]{0:T(128)} %copy-done.11) | copy-start | bytes 388
  54.4 12.0 %copy-start.6 = (bf16[1,128,128]{2,1,0:T(8,128)(2,1)S(1)}, bf16[1,128,128]{2,1,0:T(8,128)(2,1)}, u32[]{:S(2)}) copy-start(bf16[1,128,128]{2,1,0:T(8,128)(2,1)} %param.27) | copy-start | bytes 98308
  54.4 12.0 %copy-start.14 = (f32[1,128]{1,0:T(1,128)S(1)}, f32[1,128]{1,0:T(1,128)}, u32[]{:S(2)}) copy-start(f32[1,128]{1,0:T(1,128)} %param.29) | copy-start | bytes 1540
  54.4 54.2 %copy-start.16 = (f32[1,128]{1,0:T(1,128)S(1)}, f32[1,128]{1,0:T(1,128)}, u32[]{:S(2)}) copy-start(f32[1,128]{1,0:T(1,128)} %param.30) | copy-start | bytes 1540
  54.4 58.1 %copy-start.3 = (f32[4,128,1,128]{3,1,0,2:T(8,128)S(1)}, f32[4,128,1,128]{3,1,0,2:T(8,128)}, u32[]{:S(2)}) copy-start(f32[4,128,1,128]{3,1,0,2:T(8,128)} %copy-done.2) | copy-start | bytes 786436
  59.1 58.7 %copy-start.18 = (f32[1,128]{1,0:T(1,128)S(1)}, f32[1,128]{1,0:T(1,128)}, u32[]{:S(2)}) copy-start(f32[1,128]{1,0:T(1,128)} %param.31) | copy-start | bytes 1540
  59.1 53.4 %collective-permute-start.7 = (f32[4,128,128]{2,1,0:T(8,128)S(1)}, f32[4,128,128]{2,1,0:T(8,128)S(1)}, u32[]{:S(2)}, u32[]{:S(2)}) collective-permute-start(f32[4,128,128]{2,1,0:T(8,128)S(1)} %get-tuple-element.68), channel_id=1, source_target_pairs={{1,0},{2,1},{3,2},{4,3},{5,4},{6,5},{7,6},{9,8},{10,9},{11,10},{12... | collective-permute-start | bytes 786440 | tf_op jit(solution)/shard_map/ppermute | solution.py:13
  60.4 52.1 %collective-permute-start.8 = (f32[4,128,128]{2,1,0:T(8,128)S(1)}, f32[4,128,128]{2,1,0:T(8,128)S(1)}, u32[]{:S(2)}, u32[]{:S(2)}) collective-permute-start(f32[4,128,128]{2,1,0:T(8,128)S(1)} %get-tuple-element.69), channel_id=1, source_target_pairs={{0,1},{1,2},{2,3},{3,4},{4,5},{5,6},{6,7},{8,9},{9,10},{10,11},{11... | collective-permute-start | bytes 786440 | tf_op jit(solution)/shard_map/ppermute | solution.py:13
  109.5 8.3 %collective-permute-start.11 = (f32[1,128,128]{1,2,0:T(8,128)S(1)}, f32[1,128,128]{1,2,0:T(8,128)S(1)}, u32[]{:S(2)}, u32[]{:S(2)}) collective-permute-start(f32[1,128,128]{1,2,0:T(8,128)S(1)} %get-tuple-element.56), channel_id=1, source_target_pairs={{0,8},{8,16},{16,24},{24,0},{1,9},{9,17},{17,25},{25,1},{2,10},{10... | collective-permute-start | bytes 196616 | tf_op jit(solution)/shard_map/ppermute | solution.py:36
  113.4 6.0 %collective-permute-start.10 = (bf16[4,128,128]{2,1,0:T(8,128)(2,1)S(1)}, bf16[4,128,128]{2,1,0:T(8,128)(2,1)S(1)}, u32[]{:S(2)}, u32[]{:S(2)}) collective-permute-start(bf16[4,128,128]{2,1,0:T(8,128)(2,1)S(1)} %get-tuple-element.58), channel_id=1, source_target_pairs={{1,0},{2,1},{3,2},{4,3},{5,4},{6,5},{7,6},{9,8},{10,9},{11,10},{12... | collective-permute-start | bytes 393224 | tf_op jit(solution)/shard_map/ppermute | solution.py:26
  114.7 4.7 %collective-permute-start.9 = (bf16[4,128,128]{2,1,0:T(8,128)(2,1)S(1)}, bf16[4,128,128]{2,1,0:T(8,128)(2,1)S(1)}, u32[]{:S(2)}, u32[]{:S(2)}) collective-permute-start(bf16[4,128,128]{2,1,0:T(8,128)(2,1)S(1)} %get-tuple-element.58), channel_id=1, source_target_pairs={{0,1},{1,2},{2,3},{3,4},{4,5},{5,6},{6,7},{8,9},{9,10},{10,11},{11... | collective-permute-start | bytes 393224 | tf_op jit(solution)/shard_map/ppermute | solution.py:24
  122.4 2.0 %copy-start.10 = (s32[32]{0:T(128)S(1)}, s32[32]{0:T(128)}, u32[]{:S(2)}) copy-start(s32[32]{0:T(128)} %param.25) | copy-start | bytes 388
where the time goes:
time: 132 us; the launch traced here: 131 us
  blocking collectives  40.5 us (31%)
  other arithmetic  28.2 us (21%)
  starting transfers between devices  27.7 us (21%)
  local copies, waits for them, and re-layouts  16.2 us (12%)
  matrix products  11.4 us (9%)
  between operations  6.66 us (5%)
    psum x1, blocking collectives, shards(): dual_total = lax.psum(dual_sq, ('tm', 'region'))  40.5 us
    ppermute x4, starting transfers between devices, shifted(): lax.ppermute(value, axis, [(source, source + steps) for source in range(i...  11 us
    ppermute x4, starting transfers between devices, from_behind(): return lax.ppermute(value, axis, pairs)  9.8 us
    scatter-add x2, other arithmetic, pull_lines(): jax.ops.segment_sum(contrib, rel_block, num_segments=3 * line_blocks)  9.32 us
    scatter-add x2, other arithmetic, push_buses(): bus_sum = jax.ops.segment_sum(contrib, tile_bus, num_segments=bus_blocks)  5.44 us
    dot_general x2, matrix products, push_buses(): jnp.einsum('tij,tjc->tic', incid_tiles, picked, preferred_element_type=jn...  4.42 us
    ppermute x2, starting transfers between devices, with_halo(): lax.ppermute(tail, axis, [(i, (i + 1) % count) for i in range(ends)])  4.34 us
    dot_general x2, local copies, waits for them, and re-layouts, push_buses(): jnp.einsum('tij,tjc->tic', incid_tiles, picked, preferred_element_type=jn...  3.85 us
  transfers between devices with their start and end apart: 12, of which 0 were waited for; matrix products, arithmetic and copies ran while one was open for 24% of the time, Pallas kernels for 0%

commit v1 on v0

v1 whole, which is shorter than its diff:
```python
import functools

import jax
import jax.numpy as jnp
from jax import lax
from jax.experimental import pallas as pl
from jax.experimental.pallas import tpu as pltpu
from jax.sharding import PartitionSpec as P

MESH = pl.DeviceIdType.MESH
step_scale = 0.4
tiny = 1e-06
f32 = jnp.float32
bf16 = jnp.bfloat16


def remote(src, dst, send_sem, recv_sem, axis, peer):
    return pltpu.make_async_remote_copy(
        src_ref=src,
        dst_ref=dst,
        send_sem=send_sem,
        recv_sem=recv_sem,
        device_id={axis: peer},
        device_id_type=MESH,
    )


def fold(x):
    rows, columns = x.shape
    y = jnp.sum(x.reshape(rows // 8, 8, columns), axis=0)
    out = y[:, :128]
    for at in range(128, columns, 128):
        out = out + y[:, at : at + 128]
    return out


def kernel(
    dims,
    table, weight, tiles, gtiles, price, flow, gen, ramp, demand, cost, gcap, rcap, fcap,
    o_gen, o_flow, o_price, o_ramp,
    tiles_v, a_v, price_v, flow_v, gen_v, ramp_v, demand_v, cost_v, gcap_v, rcap_v, fcap_v,
    pt_v, own_v, price1_v, flow_s, gen_s, dual_s, genlow_v,
    part_send, part_recv, fw_own, fw_in, d_send, d_recv, b_send, b_recv,
    ar1_s, ar1_r, ar2_s, ar2_r,
    og_v, of_v, op_v, or_v,
    in_sem, out_sem, ps_sem, pr_sem, fs_sem, fr_sem, ds_sem, dr_sem, bs_sem, br_sem,
    a1s_sem, a1r_sem, a2s_sem, a2r_sem,
):
    nt, nr, scen, count_p, count_d = dims
    t = lax.axis_index("tm")
    r = lax.axis_index("region")
    n_tiles, blk, _ = tiles.shape
    n_gens = gtiles.shape[0]
    lines, cols = flow.shape
    buses = price.shape[0]
    lb, bb = lines // blk, buses // blk
    width = 3 * lb + n_gens
    nch = part_send.shape[2]
    cw = lines // nch
    gw = n_gens * blk

    barrier = pltpu.get_barrier_semaphore()
    for axis, me, n in (("region", r, nr), ("tm", t, nt)):
        for k in range(1, n):
            pl.semaphore_signal(
                barrier, inc=1, device_id={axis: lax.rem(me + k, n)}, device_id_type=MESH
            )

    loads = [
        pltpu.make_async_copy(src, dst, in_sem.at[i])
        for i, (src, dst) in enumerate(
            (
                (price, price_v),
                (tiles, tiles_v.at[pl.ds(0, n_tiles)]),
                (gtiles, tiles_v.at[pl.ds(n_tiles, n_gens)]),
                (ramp, ramp_v),
                (flow, flow_v),
                (gen, gen_v),
                (fcap, fcap_v),
                (cost, cost_v),
                (gcap, gcap_v),
                (rcap, rcap_v),
                (demand, demand_v),
            )
        )
    ]
    for c in loads:
        c.start()

    tiles_v[n_tiles + n_gens] = jnp.zeros((blk, blk), bf16)

    @pl.when(r == 0)
    def _():
        part_recv[:, 1] = jnp.zeros_like(part_recv[:, 1])
        fw_in[:, 0] = jnp.zeros_like(fw_in[:, 0])

    @pl.when(r == nr - 1)
    def _():
        part_recv[:, 0] = jnp.zeros_like(part_recv[:, 0])
        fw_in[:, 1] = jnp.zeros_like(fw_in[:, 1])

    has = (r > 0, r < nr - 1)
    peer = (jnp.maximum(r - 1, 0), jnp.minimum(r + 1, nr - 1))
    t_next, t_prev = lax.rem(t + 1, nt), lax.rem(t + nt - 1, nt)

    def part_copy(it, side, ch):
        return remote(
            part_send.at[it, side, ch], part_recv.at[it, side, ch],
            ps_sem.at[it, side, ch], pr_sem.at[it, side, ch], "region", peer[side],
        )

    def flow_copy(it, side, ch):
        return remote(
            fw_own.at[it, ch], fw_in.at[it, 1 - side, ch],
            fs_sem.at[it, side, ch], fr_sem.at[it, 1 - side, ch], "region", peer[side],
        )

    def dual_copy(it):
        return remote(d_send.at[it], d_recv.at[it], ds_sem.at[it], dr_sem.at[it], "tm", t_prev)

    def bar_copy(it):
        return remote(b_send.at[it], b_recv.at[it], bs_sem.at[it], br_sem.at[it], "tm", t_next)

    side_at = (0, 2 * lines)

    def build(first, count):
        for w in range(first, first + count):
            for b in range(bb):
                a_v[b * blk : (b + 1) * blk, w * blk : (w + 1) * blk] = tiles_v[table[b * width + w]]

    def pull_out(it, start_hook=None):
        for ch in range(nch):
            for side in (0, 1):
                at = side_at[side] + ch * cw
                part_send[it, side, ch] = jnp.dot(
                    pt_v[...], a_v[:, at : at + cw], preferred_element_type=f32
                )
                if start_hook is not None and ch == 0 and side == 0:
                    start_hook()

                @pl.when(has[side])
                def _():
                    part_copy(it, side, ch).start()

    def pull_own():
        own_v[:, :lines] = jnp.dot(
            pt_v[...], a_v[:, lines : 2 * lines], preferred_element_type=f32
        )
        own_v[:, lines:] = jnp.dot(
            pt_v[...], a_v[:, 3 * lines :], preferred_element_type=f32
        )

    def set_pt(ref):
        for b in range(bb):
            pt_v[:, b * blk : (b + 1) * blk] = ref[b * blk : (b + 1) * blk, :].T.astype(bf16)

    def row(ref, n):
        return jnp.concatenate([ref[i : i + 1, :] for i in range(n)], axis=1) if n > 1 else ref[...]

    def primal(it, sp):
        acc = jnp.zeros((8, 128), f32)
        per = cw // blk
        for ch in range(nch):
            for side in (0, 1):
                @pl.when(has[1 - side])
                def _():
                    part_copy(it, side, ch).wait_recv()

            lo = ch * cw
            total = own_v[:, lo : lo + cw] + part_recv[it, 0, ch] + part_recv[it, 1, ch]
            cap = jnp.concatenate(
                [fcap_v[ch * per + i : ch * per + i + 1, :] for i in range(per)], axis=1
            )
            now = flow_s[it, :, lo : lo + cw]
            new = jnp.minimum(jnp.maximum(now + sp * total, -cap), cap)
            fw_own[it, ch] = (2.0 * new - now).astype(bf16)
            for side in (0, 1):
                @pl.when(has[side])
                def _():
                    flow_copy(it, side, ch).start()
            flow_s[it + 1, :, lo : lo + cw] = new
            if it == 0:
                acc = acc + fold((new - now) ** 2)
        dual_copy(it).wait_recv()
        dual = dual_s[it]
        nxt = d_recv[it]
        later = nxt if cols == scen else jnp.concatenate([dual[scen:], nxt], axis=0)
        gnow = gen_s[it]
        grad = row(cost_v, n_gens) - own_v[:, lines:] + (dual - later)
        gnew = jnp.minimum(jnp.maximum(gnow - sp * grad, 0.0), row(gcap_v, n_gens))
        gbar = 2.0 * gnew - gnow
        b_send[it] = gbar[cols - scen :]
        bar_copy(it).start()
        gen_s[it + 1] = gnew
        genlow_v[...] = gbar.astype(bf16)
        if it == 0:
            acc = acc + fold((gnew - gnow) ** 2)
        return acc, gbar

    nt_dims = (((1,), (1,)), ((), ()))

    def push(it, finish):
        half = buses // 2
        op_v[...] = lax.dot_general(
            a_v[:, 3 * lines :], genlow_v[...], nt_dims, preferred_element_type=f32
        )
        for ch in range(nch):
            at = lines + ch * cw
            op_v[...] += lax.dot_general(
                a_v[:, at : at + cw], fw_own[it, ch], nt_dims, preferred_element_type=f32
            )
        for ch in range(nch):
            for side in (0, 1):
                @pl.when(has[side])
                def _():
                    flow_copy(it, 1 - side, ch).wait_recv()
            for side in (0, 1):
                at = side_at[side] + ch * cw
                op_v[...] += lax.dot_general(
                    a_v[:, at : at + cw], fw_in[it, side, ch], nt_dims, preferred_element_type=f32
                )

    def ramp_step(it, gbar, sd):
        bar_copy(it).wait_recv()
        prev = b_recv[it]
        earlier = prev if cols == scen else jnp.concatenate([prev, gbar[: cols - scen]], axis=0)
        dual = dual_s[it]
        lifted = dual + sd * (gbar - earlier)
        bound = row(rcap_v, n_gens)
        return lifted - sd * jnp.minimum(jnp.maximum(lifted / sd, -bound), bound)

    w1 = jnp.full((1, 1), weight[0], f32)
    loads[0].wait()
    set_pt(price_v)
    loads[1].wait()
    loads[2].wait()
    build(0, lb)
    build(2 * lb, lb)
    loads[3].wait()
    dual_s[0] = ramp_v[...].T
    d_send[0] = dual_s[0][:scen]

    def entered():
        pl.semaphore_wait(barrier, nr - 1 + nt - 1)

    pull_out(0, entered)
    dual_copy(0).start()
    build(lb, lb)
    build(3 * lb, n_gens)
    pull_own()
    for c in loads[4:]:
        c.wait()
    for b in range(lb):
        flow_s[0, :, b * blk : (b + 1) * blk] = flow_v[b * blk : (b + 1) * blk, :].T
    gen_s[0] = gen_v[...].T
    sd1 = step_scale * w1
    primal_acc, gbar1 = primal(0, step_scale / w1)
    push(0, None)
    price_one = price_v[...] + sd1 * (demand_v[...] - op_v[...])
    price1_v[...] = price_one
    dual_acc = fold((price_one - price_v[...]) ** 2)
    dual_one = ramp_step(0, gbar1, sd1)
    dual_s[1] = dual_one
    dual_acc = dual_acc + fold((dual_one - dual_s[0]) ** 2)

    ar1_s[0] = primal_acc
    ar1_s[1] = dual_acc
    first = [
        remote(ar1_s, ar1_r.at[k], a1s_sem.at[k], a1r_sem.at[k], "tm", lax.rem(t + k, nt))
        for k in range(1, nt)
    ]
    for c in first:
        c.start()
    d_send[1] = dual_one[:scen]
    set_pt(price1_v)
    pull_out(1)
    dual_copy(1).start()
    for c in first:
        c.wait_recv()
    summed = ar1_s[...]
    for k in range(1, nt):
        summed = summed + ar1_r[k]
    ar2_s[...] = summed
    second = [
        remote(ar2_s, ar2_r.at[k], a2s_sem.at[k], a2r_sem.at[k], "region", lax.rem(r + k, nr))
        for k in range(1, nr)
    ]
    for c in second:
        c.start()
    pull_own()
    for c in second:
        c.wait_recv()
    summed = ar2_s[...]
    for k in range(1, nr):
        summed = summed + ar2_r[k]
    primal_mean = jnp.sum(summed[0], keepdims=True) / count_p
    dual_mean = jnp.sum(summed[1], keepdims=True) / count_d
    w2 = jnp.sqrt(w1 * jnp.sqrt((dual_mean + tiny) / (primal_mean + tiny)))

    sd2 = step_scale * w2
    _, gbar2 = primal(1, step_scale / w2)
    for b in range(lb):
        of_v[b * blk : (b + 1) * blk, :] = flow_s[2, :, b * blk : (b + 1) * blk].T
    og_v[...] = gen_s[2].T
    outs = [
        pltpu.make_async_copy(src, dst, out_sem.at[i])
        for i, (src, dst) in enumerate(
            ((of_v, o_flow), (og_v, o_gen), (or_v, o_ramp), (price_v, o_price))
        )
    ]
    outs[0].start()
    outs[1].start()
    push(1, None)
    price_v[...] = price1_v[...] + sd2 * (demand_v[...] - op_v[...])
    outs[3].start()
    or_v[...] = ramp_step(1, gbar2, sd2).T
    outs[2].start()

    for it in range(2):
        for ch in range(nch):
            for side in (0, 1):
                @pl.when(has[side])
                def _():
                    part_copy(it, side, ch).wait_send()
                    flow_copy(it, side, ch).wait_send()
        dual_copy(it).wait_send()
        bar_copy(it).wait_send()
    for c in first + second:
        c.wait_send()
    for c in outs:
        c.wait()


def shards(
    gen, flow, price, ramp_dual, demand, incid_tiles, tile_bus, tile_line, gen_tiles, gen_bus,
    gen_cost, gen_cap, ramp_cap, flow_cap, weight,
):
    gb, blk, hours, scen = gen.shape
    lb, bb = flow.shape[0], price.shape[0]
    n_tiles = incid_tiles.shape[0]
    cols = hours * scen
    nt, nr = lax.axis_size("tm"), lax.axis_size("region")
    region = lax.axis_index("region")
    lines, buses, gens = lb * blk, bb * blk, gb * blk
    width = 3 * lb + gb
    nch = 2 if lb % 2 == 0 else 1
    cw = lines // nch

    zero_at = n_tiles + gb
    slot = tile_bus * width + (tile_line - (region - 1) * lb)
    gslot = gen_bus * width + 3 * lb + jnp.arange(gb, dtype=jnp.int32)
    places = jnp.arange(bb * width, dtype=jnp.int32)[:, None]
    ids = jnp.arange(n_tiles, dtype=jnp.int32)
    gids = n_tiles + jnp.arange(gb, dtype=jnp.int32)
    table = (
        zero_at
        + jnp.sum(jnp.where(slot == places, ids - zero_at, 0), axis=1)
        + jnp.sum(jnp.where(gslot == places, gids - zero_at, 0), axis=1)
    ).astype(jnp.int32)

    dims = (
        nt, nr, scen,
        float((gen.size + flow.size) * nt * nr), float((price.size + ramp_dual.size) * nt * nr),
    )
    any_spec = pl.BlockSpec(memory_space=pl.ANY)
    smem_spec = pl.BlockSpec(memory_space=pltpu.SMEM)
    dma = pltpu.SemaphoreType.DMA
    V = pltpu.VMEM
    scratch = [
        V((n_tiles + gb + 1, blk, blk), bf16),
        V((buses, width * blk), bf16),
        V((buses, cols), f32),
        V((lines, cols), f32),
        V((gens, cols), f32),
        V((gens, cols), f32),
        V((buses, cols), f32),
        V((gb, blk), f32),
        V((gb, blk), f32),
        V((gb, blk), f32),
        V((lb, blk), f32),
        V((cols, buses), bf16),
        V((cols, lines + gens), f32),
        V((buses, cols), f32),
        V((3, cols, lines), f32),
        V((3, cols, gens), f32),
        V((2, cols, gens), f32),
        V((cols, gens), bf16),
        V((2, 2, nch, cols, cw), f32),
        V((2, 2, nch, cols, cw), f32),
        V((2, nch, cols, cw), bf16),
        V((2, 2, nch, cols, cw), bf16),
        V((2, scen, gens), f32),
        V((2, scen, gens), f32),
        V((2, scen, gens), f32),
        V((2, scen, gens), f32),
        V((2, 8, 128), f32),
        V((nt, 2, 8, 128), f32),
        V((2, 8, 128), f32),
        V((nr, 2, 8, 128), f32),
        V((gens, cols), f32),
        V((lines, cols), f32),
        V((buses, cols), f32),
        V((gens, cols), f32),
        dma((11,)),
        dma((4,)),
        dma((2, 2, nch)),
        dma((2, 2, nch)),
        dma((2, 2, nch)),
        dma((2, 2, nch)),
        dma((2,)),
        dma((2,)),
        dma((2,)),
        dma((2,)),
        dma((nt,)),
        dma((nt,)),
        dma((nr,)),
        dma((nr,)),
    ]
    outs = pl.pallas_call(
        functools.partial(kernel, dims),
        out_shape=(
            jax.ShapeDtypeStruct((gens, cols), f32),
            jax.ShapeDtypeStruct((lines, cols), f32),
            jax.ShapeDtypeStruct((buses, cols), f32),
            jax.ShapeDtypeStruct((gens, cols), f32),
        ),
        in_specs=[smem_spec, smem_spec] + [any_spec] * 11,
        out_specs=(any_spec,) * 4,
        scratch_shapes=scratch,
        compiler_params=pltpu.CompilerParams(collective_id=0, has_side_effects=True),
    )(
        table, weight.reshape(1), incid_tiles, gen_tiles,
        price.reshape(buses, cols), flow.reshape(lines, cols), gen.reshape(gens, cols),
        ramp_dual.reshape(gens, cols), demand.reshape(buses, cols),
        gen_cost, gen_cap, ramp_cap, flow_cap,
    )
    return tuple(
        out.reshape(like.shape) for out, like in zip(outs, (gen, flow, price, ramp_dual))
    )


def solution(mesh):
    field = P("region", None, "tm", None)
    placed = (
        field, field, field, field, field,
        P("region", None, None), P("region"), P("region"), P("region", None, None), P("region"),
        P("region", None), P("region", None), P("region", None), P("region", None), P(),
    )
    return jax.shard_map(
        shards, mesh=mesh, in_specs=placed, out_specs=(field,) * 4, check_vma=False
    )
```

time: 132 us -> 35.8 us (0.27)
  blocking collectives: 40.5 us -> 0 us
  starting transfers between devices: 27.7 us -> 0 us
  other arithmetic: 28.2 us -> 0.62 us
  Pallas kernels: 0 us -> 27.5 us
  matrix products: 11.4 us -> 0 us
  local copies, waits for them, and re-layouts: 16.2 us -> 5.34 us
  between operations: 6.66 us -> 1.96 us
    psum x1 -> x0, blocking collectives: 40.5 us -> none  [shards(): dual_total = lax.psum(dual_sq, ('tm', 'region'))]
    ppermute x12 -> x0, starting transfers between devices: 27.7 us -> none  [the longest x4 11 us: shifted(): lax.ppermute(value, axis, [(source, source + steps) for source in range(i...]
    pallas_call x0 -> x1, Pallas kernels: none -> 27.5 us  [shards(): pl.pallas_call(functools.partial(kernel, dims), out_shape=(jax.ShapeDtype...]
    scatter-add x4 -> x0, other arithmetic: 14.8 us -> none  [the longest x2 9.32 us: pull_lines(): jax.ops.segment_sum(contrib, rel_block, num_segments=3 * line_blocks)]
    dot_general x8 -> x0, matrix products: 11.4 us -> none  [the longest x2 4.42 us: push_buses(): jnp.einsum('tij,tjc->tic', incid_tiles, picked, preferred_element_type=jn...]
    dot_general x4 -> x0, local copies, waits for them, and re-layouts: 7.54 us -> none  [the longest x2 3.85 us: push_buses(): jnp.einsum('tij,tjc->tic', incid_tiles, picked, preferred_element_type=jn...]
    reduce_sum x4 -> x1, other arithmetic: 6.1 us -> 0.09 us  [shards(): jnp.sum(jnp.where(slot == places, ids - zero_at, 0), axis=1)]
    gather x5 -> x0, local copies, waits for them, and re-layouts: 4.88 us -> none  [the longest x2 3.3 us: pull_lines(): picked = price_low[tile_bus]]
  transfers between devices with their start and end apart: 12 -> 0, of which waited for: 0 -> 0; matrix products, arithmetic and copies ran while one was open for 24% -> 0% of each run, Pallas kernels for 0% -> 0%
where the time goes in v1:
time: 35.8 us; the launch traced here: 35.5 us
  Pallas kernels  27.5 us (77%)
  local copies, waits for them, and re-layouts  5.34 us (15%)
  between operations  1.96 us (5%)
  other arithmetic  0.62 us (2%)
    pallas_call x1, Pallas kernels, shards(): pl.pallas_call(functools.partial(kernel, dims), out_shape=(jax.ShapeDtype...  27.5 us
    unnamed x12, local copies, waits for them, and re-layouts  5.34 us

profile of v1, /device:TPU:0, one launch (start us, length us, event | category | flops | bytes accessed | tf_op | source)
XLA Modules:
  0.0 35.5 jit_solution(9033206226860826624)
XLA Ops:
  1.9 0.0 copy-start.2
  1.9 0.0 copy-start.3
  1.9 0.6 %copy-done.2 = s32[32]{0:T(128)S(1)} copy-done((s32[32]{0:T(128)S(1)}, s32[32]{0:T(128)}, u32[]{:S(2)}) %copy-start.2) | copy-done | bytes 152
  2.6 0.0 copy-done.3
  2.6 0.1 select_reduce_fusion
  2.7 0.5 %fusion.table = s32[52]{0:T(128)} fusion(s32[52]{0:T(128)S(1)} %select_reduce_fusion, s32[]{:T(128)} %bitcast), kind=kLoop, calls=%fused_computation.3 | loop fusion | flops 208 | bytes 420 | tf_op jit(solution)/shard_map/add | solution.py:356
  3.2 27.5 %shard_map.174 = (f32[128,128]{1,0:T(8,128)}, f32[512,128]{1,0:T(8,128)}, f32[512,128]{1,0:T(8,128)}, f32[128,128]{1,0:T(8,128)}) custom-call(s32[52]{0:T(128)} %fusion.table, f32[1]{0:T(128)} %bitcast.19.weight, bf16[32,128,128]{2,1,0:T(8,128)(2,1)} %tiles.1, bf16[1,128,128]{2,1,0:T(8,128)(2,1)} %gtiles.1, f32[512,128]{1,0:T(8,128)} %bitcast.20, ...), custom_call_target="tpu_custom_call" | custom-call | tf_op jit(solution)/shard_map/pallas_call | solution.py:419
  30.8 1.5 %copy.33 = f32[1,128,1,128]{3,2,1,0:T(1,128)} copy(f32[1,128,1,128]{3,2,1,0:T(1,128)} %bitcast.28) | data formatting | bytes 131072
  32.2 0.0 copy-start
  32.3 1.7 %copy.34 = f32[4,128,1,128]{3,2,1,0:T(1,128)} copy(f32[4,128,1,128]{3,2,1,0:T(1,128)} %bitcast.24) | data formatting | bytes 524288
  34.0 0.0 copy-done
  34.0 0.0 copy-start.1
  34.0 0.7 %copy.35 = f32[4,128,1,128]{3,2,1,0:T(1,128)} copy(f32[4,128,1,128]{3,2,1,0:T(1,128)S(1)} %bitcast.23) | data formatting | bytes 524288
  34.7 0.2 copy-done.1
  34.8 0.6 %copy.36 = f32[1,128,1,128]{3,2,1,0:T(1,128)} copy(f32[1,128,1,128]{3,2,1,0:T(1,128)S(1)} %bitcast.27) | data formatting | bytes 131072
  (1 shorter events, 0.0 us)
Async XLA Ops:
  1.9 0.7 %copy-start.2 = (s32[32]{0:T(128)S(1)}, s32[32]{0:T(128)}, u32[]{:S(2)}) copy-start(s32[32]{0:T(128)} %param.22) | copy-start | bytes 388
  1.9 0.7 %copy-start.3 = (s32[32]{0:T(128)S(1)}, s32[32]{0:T(128)}, u32[]{:S(2)}) copy-start(s32[32]{0:T(128)} %param.21) | copy-start | bytes 388
  32.2 1.7 %copy-start = (f32[512,128]{1,0:T(8,128)S(1)}, f32[512,128]{1,0:T(8,128)}, u32[]{:S(2)}) copy-start(f32[512,128]{1,0:T(8,128)} %get-tuple-element.10) | copy-start | bytes 786436
  34.0 0.9 %copy-start.1 = (f32[128,128]{1,0:T(8,128)S(1)}, f32[128,128]{1,0:T(8,128)}, u32[]{:S(2)}) copy-start(f32[128,128]{1,0:T(8,128)} %get-tuple-element.11) | copy-start | bytes 196612

commit v2 on v1

--- a/solution.py
+++ b/solution.py
@@ -34,6 +34,20 @@
     return out
 
 
+def both_halves(x):
+    row = jnp.sum(x, axis=0, keepdims=True)
+    return row + pltpu.roll(row, 64, 1)
+
+
+def writer(*refs):
+    n = (len(refs) - 1) // 2
+    copies = [pltpu.make_async_copy(refs[i], refs[n + i], refs[-1].at[i]) for i in range(n)]
+    for c in copies:
+        c.start()
+    for c in copies:
+        c.wait()
+
+
 def kernel(
     dims,
     table, weight, tiles, gtiles, price, flow, gen, ramp, demand, cost, gcap, rcap, fcap,
@@ -41,10 +55,9 @@
     tiles_v, a_v, price_v, flow_v, gen_v, ramp_v, demand_v, cost_v, gcap_v, rcap_v, fcap_v,
     pt_v, own_v, price1_v, flow_s, gen_s, dual_s, genlow_v,
     part_send, part_recv, fw_own, fw_in, d_send, d_recv, b_send, b_recv,
-    ar1_s, ar1_r, ar2_s, ar2_r,
-    og_v, of_v, op_v, or_v,
-    in_sem, out_sem, ps_sem, pr_sem, fs_sem, fr_sem, ds_sem, dr_sem, bs_sem, br_sem,
-    a1s_sem, a1r_sem, a2s_sem, a2r_sem,
+    ar_s, ar_r, acc_v,
+    in_sem, ps_sem, pr_sem, fs_sem, fr_sem, ds_sem, dr_sem, bs_sem, br_sem,
+    as_sem, ar_sem, ready,
 ):
     nt, nr, scen, count_p, count_d = dims
     t = lax.axis_index("tm")
@@ -201,12 +214,12 @@
 
     def push(it, finish):
         half = buses // 2
-        op_v[...] = lax.dot_general(
+        acc_v[...] = lax.dot_general(
             a_v[:, 3 * lines :], genlow_v[...], nt_dims, preferred_element_type=f32
         )
         for ch in range(nch):
             at = lines + ch * cw
-            op_v[...] += lax.dot_general(
+            acc_v[...] += lax.dot_general(
                 a_v[:, at : at + cw], fw_own[it, ch], nt_dims, preferred_element_type=f32
             )
         for ch in range(nch):
@@ -216,7 +229,7 @@
                     flow_copy(it, 1 - side, ch).wait_recv()
             for side in (0, 1):
                 at = side_at[side] + ch * cw
-                op_v[...] += lax.dot_general(
+                acc_v[...] += lax.dot_general(
                     a_v[:, at : at + cw], fw_in[it, side, ch], nt_dims, preferred_element_type=f32
                 )
 
@@ -242,6 +255,10 @@
 
     def entered():
         pl.semaphore_wait(barrier, nr - 1 + nt - 1)
+        for k in range(1, nr):
+            pl.semaphore_signal(
+                ready, inc=1, device_id={"region": lax.rem(r + k, nr)}, device_id_type=MESH
+            )
 
     pull_out(0, entered)
     dual_copy(0).start()
@@ -256,65 +273,55 @@
     sd1 = step_scale * w1
     primal_acc, gbar1 = primal(0, step_scale / w1)
     push(0, None)
-    price_one = price_v[...] + sd1 * (demand_v[...] - op_v[...])
+    price_one = price_v[...] + sd1 * (demand_v[...] - acc_v[...])
     price1_v[...] = price_one
     dual_acc = fold((price_one - price_v[...]) ** 2)
     dual_one = ramp_step(0, gbar1, sd1)
     dual_s[1] = dual_one
     dual_acc = dual_acc + fold((dual_one - dual_s[0]) ** 2)
 
-    ar1_s[0] = primal_acc
-    ar1_s[1] = dual_acc
-    first = [
-        remote(ar1_s, ar1_r.at[k], a1s_sem.at[k], a1r_sem.at[k], "tm", lax.rem(t + k, nt))
-        for k in range(1, nt)
-    ]
-    for c in first:
+    low = lax.broadcasted_iota(jnp.int32, (1, 128), 1) < 64
+    ar_s[...] = jnp.where(low, both_halves(primal_acc), both_halves(dual_acc))
+    sums = []
+    for j in range(nt):
+        for k in range(nr):
+            if j or k:
+                at = j * nr + k
+                sums.append(
+                    pltpu.make_async_remote_copy(
+                        src_ref=ar_s,
+                        dst_ref=ar_r.at[at],
+                        send_sem=as_sem.at[at],
+                        recv_sem=ar_sem.at[at],
+                        device_id={"tm": lax.rem(t + j, nt), "region": lax.rem(r + k, nr)},
+                        device_id_type=MESH,
+                    )
+                )
+    pl.semaphore_wait(ready, nr - 1)
+    for c in sums:
         c.start()
     d_send[1] = dual_one[:scen]
     set_pt(price1_v)
     pull_out(1)
     dual_copy(1).start()
-    for c in first:
+    pull_own()
+    for c in sums:
         c.wait_recv()
-    summed = ar1_s[...]
-    for k in range(1, nt):
-        summed = summed + ar1_r[k]
-    ar2_s[...] = summed
-    second = [
-        remote(ar2_s, ar2_r.at[k], a2s_sem.at[k], a2r_sem.at[k], "region", lax.rem(r + k, nr))
-        for k in range(1, nr)
-    ]
-    for c in second:
-        c.start()
-    pull_own()
-    for c in second:
-        c.wait_recv()
-    summed = ar2_s[...]
-    for k in range(1, nr):
-        summed = summed + ar2_r[k]
-    primal_mean = jnp.sum(summed[0], keepdims=True) / count_p
-    dual_mean = jnp.sum(summed[1], keepdims=True) / count_d
+    summed = ar_s[...]
+    for at in range(1, nt * nr):
+        summed = summed + ar_r[at]
+    primal_mean = jnp.sum(jnp.where(low, summed, 0.0), axis=1, keepdims=True) / count_p
+    dual_mean = jnp.sum(jnp.where(low, 0.0, summed), axis=1, keepdims=True) / count_d
     w2 = jnp.sqrt(w1 * jnp.sqrt((dual_mean + tiny) / (primal_mean + tiny)))
 
     sd2 = step_scale * w2
     _, gbar2 = primal(1, step_scale / w2)
     for b in range(lb):
-        of_v[b * blk : (b + 1) * blk, :] = flow_s[2, :, b * blk : (b + 1) * blk].T
-    og_v[...] = gen_s[2].T
-    outs = [
-        pltpu.make_async_copy(src, dst, out_sem.at[i])
-        for i, (src, dst) in enumerate(
-            ((of_v, o_flow), (og_v, o_gen), (or_v, o_ramp), (price_v, o_price))
-        )
-    ]
-    outs[0].start()
-    outs[1].start()
+        o_flow[b * blk : (b + 1) * blk, :] = flow_s[2, :, b * blk : (b + 1) * blk].T
+    o_gen[...] = gen_s[2].T
     push(1, None)
-    price_v[...] = price1_v[...] + sd2 * (demand_v[...] - op_v[...])
-    outs[3].start()
-    or_v[...] = ramp_step(1, gbar2, sd2).T
-    outs[2].start()
+    o_price[...] = price1_v[...] + sd2 * (demand_v[...] - acc_v[...])
+    o_ramp[...] = ramp_step(1, gbar2, sd2).T
 
     for it in range(2):
         for ch in range(nch):
@@ -325,10 +332,8 @@
                     flow_copy(it, side, ch).wait_send()
         dual_copy(it).wait_send()
         bar_copy(it).wait_send()
-    for c in first + second:
+    for c in sums:
         c.wait_send()
-    for c in outs:
-        c.wait()
 
 
 def shards(
@@ -352,10 +357,12 @@
     places = jnp.arange(bb * width, dtype=jnp.int32)[:, None]
     ids = jnp.arange(n_tiles, dtype=jnp.int32)
     gids = n_tiles + jnp.arange(gb, dtype=jnp.int32)
-    table = (
+    table = jnp.clip(
         zero_at
         + jnp.sum(jnp.where(slot == places, ids - zero_at, 0), axis=1)
-        + jnp.sum(jnp.where(gslot == places, gids - zero_at, 0), axis=1)
+        + jnp.sum(jnp.where(gslot == places, gids - zero_at, 0), axis=1),
+        0,
+        zero_at,
     ).astype(jnp.int32)
 
     dims = (
@@ -393,16 +400,10 @@
         V((2, scen, gens), f32),
         V((2, scen, gens), f32),
         V((2, scen, gens), f32),
-        V((2, 8, 128), f32),
-        V((nt, 2, 8, 128), f32),
-        V((2, 8, 128), f32),
-        V((nr, 2, 8, 128), f32),
-        V((gens, cols), f32),
-        V((lines, cols), f32),
+        V((1, 128), f32),
+        V((nt * nr, 1, 128), f32),
         V((buses, cols), f32),
-        V((gens, cols), f32),
         dma((11,)),
-        dma((4,)),
         dma((2, 2, nch)),
         dma((2, 2, nch)),
         dma((2, 2, nch)),
@@ -411,21 +412,17 @@
         dma((2,)),
         dma((2,)),
         dma((2,)),
-        dma((nt,)),
-        dma((nt,)),
-        dma((nr,)),
-        dma((nr,)),
+        dma((nt * nr,)),
+        dma((nt * nr,)),
+        pltpu.SemaphoreType.REGULAR,
     ]
+    vmem_spec = pl.BlockSpec(memory_space=pltpu.VMEM)
+    shapes = ((gens, cols), (lines, cols), (buses, cols), (gens, cols))
     outs = pl.pallas_call(
         functools.partial(kernel, dims),
-        out_shape=(
-            jax.ShapeDtypeStruct((gens, cols), f32),
-            jax.ShapeDtypeStruct((lines, cols), f32),
-            jax.ShapeDtypeStruct((buses, cols), f32),
-            jax.ShapeDtypeStruct((gens, cols), f32),
-        ),
+        out_shape=tuple(V(shape, f32) for shape in shapes),
         in_specs=[smem_spec, smem_spec] + [any_spec] * 11,
-        out_specs=(any_spec,) * 4,
+        out_specs=(vmem_spec,) * 4,
         scratch_shapes=scratch,
         compiler_params=pltpu.CompilerParams(collective_id=0, has_side_effects=True),
     )(
@@ -434,6 +431,13 @@
         ramp_dual.reshape(gens, cols), demand.reshape(buses, cols),
         gen_cost, gen_cap, ramp_cap, flow_cap,
     )
+    outs = pl.pallas_call(
+        writer,
+        out_shape=tuple(jax.ShapeDtypeStruct(shape, f32) for shape in shapes),
+        in_specs=[any_spec] * 4,
+        out_specs=(any_spec,) * 4,
+        scratch_shapes=[dma((4,))],
+    )(*(pltpu.with_memory_space_constraint(out, pltpu.VMEM) for out in outs))
     return tuple(
         out.reshape(like.shape) for out, like in zip(outs, (gen, flow, price, ramp_dual))
     )

time: 35.8 us -> 29.7 us (0.83)
  local copies, waits for them, and re-layouts: 5.34 us -> 0.66 us
  Pallas kernels: 27.5 us -> 26.3 us
    unnamed x12 -> x4, local copies, waits for them, and re-layouts: 5.34 us -> 0.66 us
    pallas_call x1 -> x2, Pallas kernels: 27.5 us -> 26.3 us  [the longest x1 25.5 us: shards(): pl.pallas_call(functools.partial(kernel, dims), out_shape=tuple((V(shape,...]
    min x0 -> x1, other arithmetic: none -> 0.52 us  [shards(): jnp.clip(zero_at + jnp.sum(jnp.where(slot == places, ids - zero_at, 0), a...]
    add x1 -> x0, other arithmetic: 0.52 us -> none  [shards(): zero_at + jnp.sum(jnp.where(slot == places, ids - zero_at, 0), axis=1)]
where the time goes in v2:
time: 29.7 us; the launch traced here: 29.5 us
  Pallas kernels  26.3 us (89%)
  between operations  1.96 us (7%)
  local copies, waits for them, and re-layouts  0.66 us (2%)
  other arithmetic  0.62 us (2%)
    pallas_call x1, Pallas kernels, shards(): pl.pallas_call(functools.partial(kernel, dims), out_shape=tuple((V(shape,...  25.5 us
    pallas_call x1, Pallas kernels, shards(): pl.pallas_call(writer, out_shape=tuple((jax.ShapeDtypeStruct(shape, f32)...  0.86 us
    unnamed x4, local copies, waits for them, and re-layouts  0.66 us

profile of v2, /device:TPU:0, one launch (start us, length us, event | category | flops | bytes accessed | tf_op | source)
XLA Modules:
  0.0 29.5 jit_solution(4909658427939846670)
XLA Ops:
  1.9 0.0 copy-start
  1.9 0.0 copy-start.1
  1.9 0.6 %copy-done = s32[32]{0:T(128)S(1)} copy-done((s32[32]{0:T(128)S(1)}, s32[32]{0:T(128)}, u32[]{:S(2)}) %copy-start) | copy-done | bytes 152
  2.6 0.0 copy-done.1
  2.6 0.1 select_reduce_fusion
  2.7 0.5 %fusion.1.table = s32[52]{0:T(128)} fusion(s32[52]{0:T(128)S(1)} %select_reduce_fusion, s32[]{:T(128)} %bitcast), kind=kLoop, calls=%fused_computation.4 | loop fusion | flops 260 | bytes 420 | tf_op jit(solution)/shard_map/jit(clip)/min | solution.py:360
  3.2 25.5 %shard_map.174 = (f32[128,128]{1,0:T(8,128)S(1)}, f32[512,128]{1,0:T(8,128)S(1)}, f32[512,128]{1,0:T(8,128)S(1)}, f32[128,128]{1,0:T(8,128)S(1)}) custom-call(s32[52]{0:T(128)} %fusion.1.table, f32[1]{0:T(128)} %bitcast.19.weight, bf16[32,128,128]{2,1,0:T(8,128)(2,1)} %tiles.1, bf16[1,128,128]{2,1,0:T(8,128)(2,1)} %gtiles.1, f32[512,128]{1,0:T(8,128)} %bitcast.20, ...), custom_call_target="tpu_custom_call" | custom-call | tf_op jit(solution)/shard_map/pallas_call | solution.py:421
  28.7 0.9 %shard_map.175 = (f32[128,128]{1,0:T(8,128)}, f32[512,128]{1,0:T(8,128)}, f32[512,128]{1,0:T(8,128)}, f32[128,128]{1,0:T(8,128)}) custom-call(f32[128,128]{1,0:T(8,128)S(1)} %get-tuple-element.12.refs_0_, f32[512,128]{1,0:T(8,128)S(1)} %get-tuple-element.13.refs_1_, f32[512,128]{1,0:T(8,128)S(1)} %get-tuple-element.14.refs_2_, ...), custom_call_target="tpu_custom_call" | custom-call | tf_op jit(solution)/shard_map/pallas_call | solution.py:434
  (1 shorter events, 0.0 us)
Async XLA Ops:
  1.9 0.7 %copy-start = (s32[32]{0:T(128)S(1)}, s32[32]{0:T(128)}, u32[]{:S(2)}) copy-start(s32[32]{0:T(128)} %param.22) | copy-start | bytes 388
  1.9 0.7 %copy-start.1 = (s32[32]{0:T(128)S(1)}, s32[32]{0:T(128)}, u32[]{:S(2)}) copy-start(s32[32]{0:T(128)} %param.21) | copy-start | bytes 388

commit v3 on v2

--- a/solution.py
+++ b/solution.py
@@ -50,14 +50,14 @@
 
 def kernel(
     dims,
-    table, weight, tiles, gtiles, price, flow, gen, ramp, demand, cost, gcap, rcap, fcap,
+    gen_bus, weight, tile_bus, tile_line, tiles, gtiles, price, flow, gen, ramp, demand, cost, gcap, rcap, fcap,
     o_gen, o_flow, o_price, o_ramp,
     tiles_v, a_v, price_v, flow_v, gen_v, ramp_v, demand_v, cost_v, gcap_v, rcap_v, fcap_v,
     pt_v, own_v, price1_v, flow_s, gen_s, dual_s, genlow_v,
     part_send, part_recv, fw_own, fw_in, d_send, d_recv, b_send, b_recv,
-    ar_s, ar_r, acc_v,
+    ar_s, ar_r, acc_v, bus_v, line_v, table_v, table_s,
     in_sem, ps_sem, pr_sem, fs_sem, fr_sem, ds_sem, dr_sem, bs_sem, br_sem,
-    as_sem, ar_sem, ready,
+    as_sem, ar_sem, ready, table_sem,
 ):
     nt, nr, scen, count_p, count_d = dims
     t = lax.axis_index("tm")
@@ -83,6 +83,8 @@
         pltpu.make_async_copy(src, dst, in_sem.at[i])
         for i, (src, dst) in enumerate(
             (
+                (tile_bus, bus_v),
+                (tile_line, line_v),
                 (price, price_v),
                 (tiles, tiles_v.at[pl.ds(0, n_tiles)]),
                 (gtiles, tiles_v.at[pl.ds(n_tiles, n_gens)]),
@@ -139,7 +141,7 @@
     def build(first, count):
         for w in range(first, first + count):
             for b in range(bb):
-                a_v[b * blk : (b + 1) * blk, w * blk : (w + 1) * blk] = tiles_v[table[b * width + w]]
+                a_v[b * blk : (b + 1) * blk, w * blk : (w + 1) * blk] = tiles_v[table_s[0, b * width + w]]
 
     def pull_out(it, start_hook=None):
         for ch in range(nch):
@@ -242,14 +244,32 @@
         bound = row(rcap_v, n_gens)
         return lifted - sd * jnp.minimum(jnp.maximum(lifted / sd, -bound), bound)
 
+    zero_at = n_tiles + n_gens
+    loads[0].wait()
+    loads[1].wait()
+    slot = bus_v[...] * width + (line_v[...] - (r - 1) * lb)
+    down = lax.broadcasted_iota(jnp.int32, (n_tiles, n_tiles), 0)
+    across = lax.broadcasted_iota(jnp.int32, (n_tiles, n_tiles), 1)
+    upright = jnp.sum(jnp.where(down == across, slot, 0), axis=1, keepdims=True)
+    places = lax.broadcasted_iota(jnp.int32, (n_tiles, 128), 1)
+    ids = lax.broadcasted_iota(jnp.int32, (n_tiles, 128), 0)
+    found = jnp.sum(jnp.where(upright == places, ids - zero_at, 0), axis=0, keepdims=True)
+    lane = lax.broadcasted_iota(jnp.int32, (1, 128), 1)
+    for g in range(n_gens):
+        found = jnp.where(lane == gen_bus[g] * width + 3 * lb + g, n_tiles + g - zero_at, found)
+    table_v[...] = jnp.clip(zero_at + found, 0, zero_at)
+    to_scalar = pltpu.make_async_copy(table_v, table_s, table_sem.at[0])
+    to_scalar.start()
+
     w1 = jnp.full((1, 1), weight[0], f32)
-    loads[0].wait()
+    loads[2].wait()
     set_pt(price_v)
-    loads[1].wait()
-    loads[2].wait()
+    loads[3].wait()
+    loads[4].wait()
+    to_scalar.wait()
     build(0, lb)
     build(2 * lb, lb)
-    loads[3].wait()
+    loads[5].wait()
     dual_s[0] = ramp_v[...].T
     d_send[0] = dual_s[0][:scen]
 
@@ -265,7 +285,7 @@
     build(lb, lb)
     build(3 * lb, n_gens)
     pull_own()
-    for c in loads[4:]:
+    for c in loads[6:]:
         c.wait()
     for b in range(lb):
         flow_s[0, :, b * blk : (b + 1) * blk] = flow_v[b * blk : (b + 1) * blk, :].T
@@ -345,25 +365,10 @@
     n_tiles = incid_tiles.shape[0]
     cols = hours * scen
     nt, nr = lax.axis_size("tm"), lax.axis_size("region")
-    region = lax.axis_index("region")
     lines, buses, gens = lb * blk, bb * blk, gb * blk
     width = 3 * lb + gb
     nch = 2 if lb % 2 == 0 else 1
     cw = lines // nch
-
-    zero_at = n_tiles + gb
-    slot = tile_bus * width + (tile_line - (region - 1) * lb)
-    gslot = gen_bus * width + 3 * lb + jnp.arange(gb, dtype=jnp.int32)
-    places = jnp.arange(bb * width, dtype=jnp.int32)[:, None]
-    ids = jnp.arange(n_tiles, dtype=jnp.int32)
-    gids = n_tiles + jnp.arange(gb, dtype=jnp.int32)
-    table = jnp.clip(
-        zero_at
-        + jnp.sum(jnp.where(slot == places, ids - zero_at, 0), axis=1)
-        + jnp.sum(jnp.where(gslot == places, gids - zero_at, 0), axis=1),
-        0,
-        zero_at,
-    ).astype(jnp.int32)
 
     dims = (
         nt, nr, scen,
@@ -403,7 +408,11 @@
         V((1, 128), f32),
         V((nt * nr, 1, 128), f32),
         V((buses, cols), f32),
-        dma((11,)),
+        V((1, n_tiles), jnp.int32),
+        V((1, n_tiles), jnp.int32),
+        V((1, 128), jnp.int32),
+        pltpu.SMEM((1, 128), jnp.int32),
+        dma((13,)),
         dma((2, 2, nch)),
         dma((2, 2, nch)),
         dma((2, 2, nch)),
@@ -415,18 +424,19 @@
         dma((nt * nr,)),
         dma((nt * nr,)),
         pltpu.SemaphoreType.REGULAR,
+        dma((1,)),
     ]
     vmem_spec = pl.BlockSpec(memory_space=pltpu.VMEM)
     shapes = ((gens, cols), (lines, cols), (buses, cols), (gens, cols))
     outs = pl.pallas_call(
         functools.partial(kernel, dims),
         out_shape=tuple(V(shape, f32) for shape in shapes),
-        in_specs=[smem_spec, smem_spec] + [any_spec] * 11,
+        in_specs=[smem_spec, smem_spec] + [any_spec] * 13,
         out_specs=(vmem_spec,) * 4,
         scratch_shapes=scratch,
         compiler_params=pltpu.CompilerParams(collective_id=0, has_side_effects=True),
     )(
-        table, weight.reshape(1), incid_tiles, gen_tiles,
+        gen_bus, weight.reshape(1), tile_bus.reshape(1, n_tiles), tile_line.reshape(1, n_tiles), incid_tiles, gen_tiles,
         price.reshape(buses, cols), flow.reshape(lines, cols), gen.reshape(gens, cols),
         ramp_dual.reshape(gens, cols), demand.reshape(buses, cols),
         gen_cost, gen_cap, ramp_cap, flow_cap,

time: 29.7 us -> 27.8 us (0.936)
  local copies, waits for them, and re-layouts: 0.66 us -> 0 us
  other arithmetic: 0.62 us -> 0 us
  Pallas kernels: 26.3 us -> 25.7 us
    unnamed x4 -> x0, local copies, waits for them, and re-layouts: 0.66 us -> none
    pallas_call x1, Pallas kernels: 25.5 us -> 24.8 us  [shards(): pl.pallas_call(functools.partial(kernel, dims), out_shape=tuple((V(shape,...]
    min x1 -> x0, other arithmetic: 0.52 us -> none  [shards(): jnp.clip(zero_at + jnp.sum(jnp.where(slot == places, ids - zero_at, 0), a...]
where the time goes in v3:
time: 27.8 us; the launch traced here: 27.6 us
  Pallas kernels  25.7 us (92%)
  between operations  1.94 us (7%)
    pallas_call x1, Pallas kernels, shards(): pl.pallas_call(functools.partial(kernel, dims), out_shape=tuple((V(shape,...  24.8 us
    pallas_call x1, Pallas kernels, shards(): pl.pallas_call(writer, out_shape=tuple((jax.ShapeDtypeStruct(shape, f32)...  0.86 us

profile of v3, /device:TPU:0, one launch (start us, length us, event | category | flops | bytes accessed | tf_op | source)
XLA Modules:
  0.0 27.6 jit_solution(1890729676615691392)
XLA Ops:
  1.9 24.8 %shard_map.174 = (f32[128,128]{1,0:T(8,128)S(1)}, f32[512,128]{1,0:T(8,128)S(1)}, f32[512,128]{1,0:T(8,128)S(1)}, f32[128,128]{1,0:T(8,128)S(1)}) custom-call(s32[1]{0:T(128)S(6)} %copy.23.gen_bus, f32[1]{0:T(128)} %bitcast.20.weight, s32[1,32]{1,0:T(1,128)} %bitcast.26, s32[1,32]{1,0:T(1,128)} %bitcast.27, bf16[32,128,128]{2,1,0:T(8,128)(2,1)} %tiles.1, ...), custom_call_target="tpu_custom_call" | custom-call | tf_op jit(solution)/shard_map/pallas_call | solution.py:431
  26.8 0.9 %shard_map.175 = (f32[128,128]{1,0:T(8,128)}, f32[512,128]{1,0:T(8,128)}, f32[512,128]{1,0:T(8,128)}, f32[128,128]{1,0:T(8,128)}) custom-call(f32[128,128]{1,0:T(8,128)S(1)} %get-tuple-element.12.refs_0_, f32[512,128]{1,0:T(8,128)S(1)} %get-tuple-element.13.refs_1_, f32[512,128]{1,0:T(8,128)S(1)} %get-tuple-element.14.refs_2_, ...), custom_call_target="tpu_custom_call" | custom-call | tf_op jit(solution)/shard_map/pallas_call | solution.py:444
